TPU v7x, 512 devices: a whole 4x4x16 slice. The times are simulated.
512 devices in a mesh: layer: 8 (over z_hi, y), feat: 64 (over x, z_lo, core).
Axes of the slice: x: 4, y: 4, z: 16 (z_hi: 2, z_lo: 8; z = z_hi * 8 + z_lo), core: 2. Of those that a mesh axis runs over, the one named last changes fastest.
Arguments:
- residual: bfloat16 [8, 256, 4096], P('layer', 'feat'), may hold values from -6 to 6
- targets: bfloat16 [8, 256, 4096], P('layer', 'feat'), may hold values from -6 to 6
- w_enc: bfloat16 [8, 4096, 8192], P('layer', None, 'feat'), may hold values from -0.09375 to 0.09375
- b_enc: float32 [8, 8192], P('layer', 'feat'), may hold values from -3 to 3
- w_dec: bfloat16 [8, 8192, 4096], P('layer', 'feat'), may hold values from -0.0625 to 0.0625
- block_mask: int32 [8, 2, 64], P('layer', None, 'feat'), may hold values from 0 to 1, as said below
Outputs:
- grad_encoder: bfloat16 [8, 4096, 8192], P('layer', None, 'feat')
- grad_bias: float32 [8, 8192], P('layer', 'feat')
- grad_decoder: bfloat16 [8, 8192, 4096], P('layer', 'feat')
- loss: float32 [], replicated
Inputs may be any that keep to these rules, and one draw needn't show every extreme that they name: `block_mask`: each feature block of a layer has its own activity level, so the number of active blocks differs from device to device; some feature blocks are never active and some always.
All inputs are finite; a program needn't handle non-finite values.
Results may differ from a plain program's by a relative error of at most 0.0056.
Values may be sent and summed in bfloat16 or wider, within the bound.
A program may use at most 64 MiB of HBM per device.

v0:
```python
import jax
import jax.numpy as jnp
from jax import lax
from jax.sharding import PartitionSpec as P

TBLOCK = 128
FBLOCK = 128


penalty_weight = 0.5
norm_epsilon = 1e-06


def shifted(block, axis, distance):
    devices = range(lax.axis_size(axis))
    route = [((i - distance) % len(devices), i) for i in devices]
    return lax.ppermute(block, axis, route)


def contract_rows(left, right):
    return lax.dot_general(
        left, right, (((0,), (0,)), ((), ())), preferred_element_type=jnp.float32
    )


def body(residual, targets, w_enc, b_enc, w_dec, block_mask):
    own_rows = residual[0]
    encoder = w_enc[0]
    enc_bias = b_enc[0]
    decoder = w_dec[0]
    blocks = block_mask[0]
    row_count = own_rows.shape[0]
    width = own_rows.shape[1]
    layers = lax.axis_size("layer")
    tokens = row_count * lax.axis_size("feat")
    keep_mask = jnp.repeat(jnp.repeat(blocks, TBLOCK, axis=0), FBLOCK, axis=1).astype(jnp.float32)
    gathered = lax.all_gather(own_rows, "feat", axis=0, tiled=True)
    preact = jnp.dot(gathered, encoder, preferred_element_type=jnp.float32) + enc_bias
    positive = jnp.maximum(preact, 0.0)
    activation = (keep_mask * positive * positive).astype(jnp.bfloat16)
    act_float = activation.astype(jnp.float32)
    row_norms = jnp.sqrt(jnp.sum(jnp.square(decoder.astype(jnp.float32)), axis=1) + norm_epsilon)
    penalty_local = jnp.sum(act_float * row_norms[None, :])
    act_rows = activation
    recon_rows = lax.psum_scatter(
        jnp.dot(act_rows, decoder, preferred_element_type=jnp.float32),
        "feat",
        scatter_dimension=0,
        tiled=True,
    )
    owned = shifted(recon_rows, "layer", 1)
    misfit = owned - targets[0].astype(jnp.float32)
    error_back = shifted(misfit.astype(jnp.bfloat16), "layer", -1)
    square_local = jnp.sum(misfit * misfit)
    shard_rows = lax.all_gather(error_back, "feat", axis=0, tiled=True)
    act_rows = activation
    dec_total = contract_rows(act_rows, shard_rows)
    grad_rows = lax.dot_general(
        shard_rows, decoder, (((1,), (1,)), ((), ())), preferred_element_type=jnp.float32
    )
    dec_grad = dec_total
    act_grad = grad_rows
    act_sum = jnp.sum(act_float, axis=0)
    dec_grad = (
        dec_grad
        + penalty_weight * act_sum[:, None] * decoder.astype(jnp.float32) / row_norms[:, None]
    )
    act_grad = act_grad + penalty_weight * row_norms[None, :]
    pre_grad = (act_grad * keep_mask * 2.0 * positive).astype(jnp.bfloat16)
    bias_grad = jnp.sum(pre_grad.astype(jnp.float32), axis=0)
    enc_grad = contract_rows(gathered, pre_grad)
    square_sum, penalty_sum = lax.psum((square_local, penalty_local), ("layer", "feat"))
    loss = (0.5 * square_sum + penalty_weight * penalty_sum) / (layers * tokens * width)
    return (
        enc_grad.astype(jnp.bfloat16)[None],
        bias_grad[None],
        dec_grad.astype(jnp.bfloat16)[None],
        loss,
    )


def solution(mesh):
    return jax.shard_map(
        body,
        mesh=mesh,
        in_specs=(
            P("layer", "feat", None),
            P("layer", "feat", None),
            P("layer", None, "feat"),
            P("layer", "feat"),
            P("layer", "feat", None),
            P("layer", None, "feat"),
        ),
        out_specs=(P("layer", None, "feat"), P("layer", "feat"), P("layer", "feat", None), P()),
        check_vma=False,
    )
```

profile of v0, /device:TPU:1, one launch (start us, length us, event | category | flops | bytes accessed | tf_op | source)
XLA Modules:
  0.0 1157.0 jit_solution(10329665504624032497)
XLA Ops:
  7.2 0.0 copy-start
  7.2 0.0 all-gather.5.cloned.1.call-start
  7.2 1.5 copy.13
  8.7 0.0 all-gather.5.cloned.1.call-update
  8.8 0.0 all-reduce.3.cloned.1.call-start
  8.8 1.5 fusion.3
  10.3 0.7 convert_bitcast_fusion
  11.0 0.1 broadcast_bitcast_fusion
  11.1 128.0 %all-gather.5.cloned.1.call-done = bf16[1,256,4096]{2,0,1:T(2,128)(2,1)} async-done(((bf16[1,4,4096]{2,0,1:T(2,128)(2,1)}), bf16[1,256,4096]{2,0,1:T(2,128)(2,1)}) %all-gather.5.cloned.1.call-update) | async-done | bytes 2097168 | tf_op jit(solution)/shard_map/all_gather | solution.py:37
  139.1 0.0 copy-done
  139.1 5.4 fusion.24
  144.5 0.0 copy-done.1
  144.5 2.7 fusion.19
  147.2 0.0 all-reduce.3.cloned.1.call-update
  147.2 0.0 all-gather.7.cloned.1.call-start
  147.2 1.3 dynamic-slice
  149.2 839.3 %all-reduce.3.cloned.1.call-done = f32[256,4096]{1,0:T(8,128)} async-done(((f32[256,4096]{1,0:T(8,128)}), f32[256,4096]{1,0:T(8,128)}) %all-reduce.3.cloned.1.call-update) | async-done | bytes 4194320
  988.5 0.9 constant_dynamic-slice_fusion
  989.4 3.2 collective-permute-start
  992.6 12.6 %collective-permute-done = f32[4,4096]{1,0:T(4,128)S(1)} collective-permute-done((f32[4,4096]{1,0:T(4,128)S(1)}, f32[4,4096]{1,0:T(4,128)S(1)}, u32[]{:S(2)}, u32[]{:S(2)}) %collective-permute-start) | collective-permute-done | bytes 65568 | tf_op jit(solution)/shard_map/ppermute | solution.py:17
  1005.3 0.6 multiply_reduce_fusion
  1005.9 1.9 collective-permute-start.1
  1007.8 2.7 collective-permute-done.1
  1010.5 0.6 copy-done.2
  1011.2 0.0 all-gather.7.cloned.1.call-update
  1012.5 110.9 %psum.16 = f32[]{:T(128)} all-reduce(f32[]{:T(128)S(6)} %mul.75), channel_id=1, replica_groups=mesh['layer'=8,'feat'=64] {'layer','feat'}, use_global_device_ids=true, to_apply=%region_5.0 | all-reduce | flops 1 | bytes 8 | tf_op jit(solution)/shard_map/psum | solution.py:72
  1124.1 9.3 all-gather.7.cloned.1.call-done
  1133.4 4.0 reshape.41
  1137.3 2.8 convert_reduce_fusion.1
  1140.2 4.7 fusion.2
  1144.8 1.3 copy.14
  1146.2 3.2 fusion.1
  (6 shorter events, 0.0 us)
Async XLA Ops:
  7.2 131.9 %copy-start = (bf16[1,4096,128]{2,1,0:T(8,128)(2,1)S(1)}, bf16[1,4096,128]{2,1,0:T(8,128)(2,1)}, u32[]{:S(2)}) copy-start(bf16[1,4096,128]{2,1,0:T(8,128)(2,1)} %param.8) | copy-start | bytes 3145732
  7.2 131.9 %all-gather.5.cloned.1.call-start = ((), (), s32[]{:S(2)}) async-start(), calls=%async_computation | async-start | bytes 4259840 | tf_op jit(solution)/shard_map/all_gather | solution.py:37
  8.8 979.7 %all-reduce.3.cloned.1.call-start = ((), (), s32[]{:S(2)}) async-start(), calls=%async_computation.2 | async-start | bytes 8388608
  139.1 5.4 copy-start.1
  147.2 858.1 %copy-start.3 = (bf16[1,4,4096]{2,1,0:T(4,128)(2,1)S(1)}, bf16[1,4,4096]{2,1,0:T(4,128)(2,1)}, u32[]{:S(2)}) copy-start(bf16[1,4,4096]{2,1,0:T(4,128)(2,1)} %param.7) | copy-start | bytes 98308
  147.2 986.2 %all-gather.7.cloned.1.call-start = ((), (), s32[]{:S(2)}) async-start(), calls=%async_computation.1 | async-start | bytes 2129920 | tf_op jit(solution)/shard_map/all_gather | solution.py:55
  989.4 15.8 %collective-permute-start = (f32[4,4096]{1,0:T(4,128)S(1)}, f32[4,4096]{1,0:T(4,128)S(1)}, u32[]{:S(2)}, u32[]{:S(2)}) collective-permute-start(f32[4,4096]{1,0:T(4,128)S(1)} %constant_dynamic-slice_fusion), channel_id=1, source_target_pairs={{448,0},{0,64},{64,128},{128,192},{192,256},{256,320},{320,384},{3... | collective-permute-start | bytes 196616 | tf_op jit(solution)/shard_map/ppermute | solution.py:17
  1005.9 4.6 collective-permute-start.1
  1010.5 0.6 copy-start.2
Sparse Core Ops, SparseCore 0:
  10.7 128.3 all-gather.4
  147.3 841.1 all-reduce.2
  1011.3 122.0 all-gather.6
where the time goes:
time: 1160 us
  waiting for transfers between devices  992 us (86%)
  blocking collectives  111 us (10%)
  matrix products  18.8 us (2%)
  between operations  17.5 us (2%)
    unnamed x4, waiting for transfers between devices  839 us
    all_gather x1, waiting for transfers between devices, body(): gathered = lax.all_gather(own_rows, 'feat', axis=0, tiled=True)  128 us
    psum x1, blocking collectives, body(): lax.psum((square_local, penalty_local), ('layer', 'feat'))  111 us
  transfers between devices with their start and end apart: 5, of which 5 were waited for; matrix products, arithmetic and copies ran while one was open for 0% of the time, Pallas kernels for 0%

commit v1 on v0

v1 whole, which is shorter than its diff:
```python
import jax
import jax.numpy as jnp
from jax import lax
from jax.experimental import pallas as pl
from jax.experimental.pallas import tpu as pltpu
from jax.sharding import PartitionSpec as P

NX, NZ, NC, NY = 4, 8, 2, 4
TOKENS, D, FD = 256, 4096, 128
SL = D // NX
CORE_ROWS = TOKENS // NC
HALF = CORE_ROWS // 2
PR = CORE_ROWS // NZ
CHUNKS = 2
CW = SL // CHUNKS
COPIES = 256

penalty_weight = 0.5
norm_epsilon = 1e-06
f32, bf16 = jnp.float32, jnp.bfloat16


def contract_last(a, b):
    return lax.dot_general(a, b, (((1,), (1,)), ((), ())), preferred_element_type=f32)


def fold(v):
    total = None
    for r in range(0, v.shape[0], 8):
        for q in range(0, v.shape[1], 128):
            tile = v[r : r + 8, q : q + 128]
            total = tile if total is None else total + tile
    return total


def kernel(
    scale,
    mask_ref, res_ref, tgt_ref, wenc_hbm, benc_ref, wdec_hbm,
    enc_out, bias_out, dec_out, loss_out,
    raw, traw, tp, tsh, tsw, tfin, g, gt, bk, wenc, wcat, act, actcat, pos2, part, own,
    opl, opr, accr, accl, inl, inr, sumb, ssum, za, zb, zc, zr, lossb, lsend, lrecv, lz, norms, actg,
    decb, encb, send, recv, local,
):
    layer = lax.axis_index("layer")
    feat = lax.axis_index("feat")
    zh, y = layer // NY, lax.rem(layer, NY)
    c = lax.rem(feat, NC)
    z = lax.rem(feat // NC, NZ)
    x = feat // (NC * NZ)
    h, zq = z // 4, lax.rem(z, 4)
    xr, xo, xl = (lax.rem(x + d, NX) for d in (1, 2, 3))

    def dev(l=layer, xx=x, zz=z, cc=c):
        return (l, (xx * NZ + zz) * NC + cc)

    zpeers = [h * 4 + lax.rem(zq + d, 4) for d in range(4)]
    zfrom = [h * 4 + lax.rem(zq + 4 - d, 4) for d in range(4)]
    zx = lax.rem(z + 4, NZ)
    zphys = zh * NZ + z

    def far(step):
        zz = lax.rem(zphys + step, 2 * NZ)
        return dev((zz // NZ) * NY + y, x, lax.rem(zz, NZ))

    up, down = far(4), far(12)
    ydn = dev(zh * NY + lax.rem(y + 3, NY))
    yup = dev(zh * NY + lax.rem(y + 1, NY))
    mate = dev(cc=1 - c)
    right, left, opp = dev(xx=xr), dev(xx=xl), dev(xx=xo)

    used = [0]
    sends = []

    class Remote:
        def __init__(self, device):
            self.i, self.device = used[0], device
            used[0] += 1

        def go(self, src, dst, keep=True):
            d = pltpu.make_async_remote_copy(
                src, dst, send.at[self.i], recv.at[self.i],
                device_id=self.device, device_id_type=pl.DeviceIdType.MESH,
            )
            d.start()
            if keep:
                sends.append(d)
            return d

        def wait(self, landed):
            pltpu.make_async_remote_copy(
                landed, landed, send.at[self.i], recv.at[self.i],
                device_id=self.device, device_id_type=pl.DeviceIdType.MESH,
            ).wait_recv()

    wrow = pl.multiple_of(c * FD, FD)
    orow = pl.multiple_of((1 - c) * FD, FD)
    load_dec = pltpu.make_async_copy(wdec_hbm.at[0], wcat.at[pl.ds(wrow, FD)], local.at[0])
    load_enc = pltpu.make_async_copy(wenc_hbm.at[0], wenc, local.at[1])
    load_dec.start()
    load_enc.start()

    barrier = pltpu.get_barrier_semaphore()
    partners = [mate, right, left, opp, *(dev(zz=q) for q in zpeers[1:]), up, down, yup, ydn]
    for p in partners:
        pl.semaphore_signal(barrier, inc=1, device_id=p, device_id_type=pl.DeviceIdType.MESH)
    pl.semaphore_wait(barrier, len(partners))

    rows_c = c * CORE_ROWS

    def slab(xx):
        return pl.ds(pl.multiple_of(xx * SL, SL), SL)

    xdevs = {1: (right, xr), 2: (opp, xo), 3: (left, xl)}

    def stage0(src, buf, sem):
        rem = {}
        for d in (2, 1, 3):
            device, xx = xdevs[d]
            rem[d] = Remote(device)
            rem[d].go(src.at[0, :, slab(xx)], buf.at[x])
        mine = pltpu.make_async_copy(src.at[0, :, slab(x)], buf.at[x], local.at[sem])
        mine.start()

        def finish():
            mine.wait()
            for d in (1, 3, 2):
                rem[d].wait(buf.at[lax.rem(x + 4 - d, NX)])
            return jnp.concatenate([buf[i].astype(f32) for i in range(NX)], axis=0).astype(bf16)

        return finish

    res_done = stage0(res_ref, raw, 2)
    tgt_done = stage0(tgt_ref, traw, 3)

    def gather(buf, k):
        def rows(first, n, xx):
            return buf.at[
                pl.ds(pl.multiple_of(first, 16), n),
                pl.ds(pl.multiple_of(xx * SL + k * CW, CW), CW),
            ]

        def piece(zz):
            return rows(rows_c + zz * PR, PR, x)

        def half(hh, xx, cc=c):
            return rows(cc * CORE_ROWS + hh * HALF, HALF, xx)

        def quarter(hh, s, xx, cc=c):
            return rows(cc * CORE_ROWS + hh * HALF + s * (HALF // 2), HALF // 2, xx)

        z1 = [None] + [Remote(dev(zz=zpeers[d])) for d in (1, 2, 3)]
        zcr = Remote(dev(zz=zx))
        z2 = [None] + [Remote(dev(zz=zpeers[d])) for d in (1, 2, 3)]
        xrt = [Remote(right) for _ in range(2)]
        xlt = [Remote(left) for _ in range(2)]
        frt = [Remote(right) for _ in range(2)]
        flt = [Remote(left) for _ in range(2)]
        mates = []

        def hand(which, at, *key):
            m = Remote(mate)
            src = which(*key, at)
            m.go(src, src)
            mates.append((m, which, key, at))

        zcr.go(piece(z), piece(z))
        for d in (2, 1, 3):
            z1[d].go(piece(z), piece(z))
        yield
        for d in (1, 2, 3):
            z1[d].wait(piece(zfrom[d]))
        xrt[0].go(half(h, x), half(h, x))
        xlt[0].go(half(h, x), half(h, x))
        hand(half, x, h)
        yield
        zcr.wait(piece(zx))
        for d in (2, 1, 3):
            z2[d].go(piece(zx), piece(zx))
        yield
        o = 1 - h
        for d in (1, 2, 3):
            z2[d].wait(piece(lax.rem(zfrom[d] + 4, NZ)))
        xrt[1].go(half(o, x), half(o, x))
        xlt[1].go(half(o, x), half(o, x))
        hand(half, x, o)
        for i, hh in enumerate((h, o)):
            yield
            xrt[i].wait(half(hh, xl))
            frt[i].go(quarter(hh, 0, xl), quarter(hh, 0, xl))
            hand(half, xl, hh)
            xlt[i].wait(half(hh, xr))
            flt[i].go(quarter(hh, 1, xr), quarter(hh, 1, xr))
            hand(half, xr, hh)
        yield
        for i, hh in enumerate((h, o)):
            frt[i].wait(quarter(hh, 0, xo))
            hand(quarter, xo, hh, 0)
            flt[i].wait(quarter(hh, 1, xo))
            hand(quarter, xo, hh, 1)
        yield
        for m, which, key, at in mates:
            m.wait(which(*key, at, 1 - c))

    load_dec.wait()
    wd = Remote(mate)
    wd.go(wcat.at[pl.ds(wrow, FD)], wcat.at[pl.ds(wrow, FD)])

    first = res_done()
    g[pl.ds(pl.multiple_of(rows_c + z * PR, PR), PR), slab(x)] = first
    gathers = [gather(g, k) for k in range(CHUNKS)]

    def step(*gens):
        for gen in gens:
            next(gen, None)

    step(*gathers)

    tp[...] = tgt_done()
    shift = Remote(ydn)
    shift.go(tp, tsh)

    sq = jnp.zeros((FD, 128), f32)
    for q in range(0, D, 512):
        w = wcat[pl.ds(wrow, FD), q : q + 512].astype(f32)
        w = w * w
        sq = sq + (w[:, :128] + w[:, 128:256]) + (w[:, 256:384] + w[:, 384:])
    norm_col = jnp.sqrt(jnp.sum(sq, axis=1, keepdims=True) + norm_epsilon)
    norms[...] = jnp.broadcast_to(norm_col, (FD, FD)).T

    step(*gathers)
    step(*gathers)

    shift.wait(tsh)
    swap1, swap2 = Remote(up), Remote(up)
    edge = y == NY - 1

    @pl.when(edge)
    def _():
        swap1.go(tsh, tsw.at[0], keep=False)

    for _ in range(3):
        step(*gathers)

    @pl.when(edge)
    def _():
        swap1.wait(tsw.at[0])
        swap2.go(tsw.at[0], tsw.at[1], keep=False)

    for _ in range(3):
        step(*gathers)

    load_enc.wait()
    pre = jnp.dot(g[...], wenc[...], preferred_element_type=f32) + benc_ref[...]
    positive = jnp.maximum(pre, 0.0)
    at = lax.broadcasted_iota(jnp.int32, (TOKENS, FD), 0)
    keep = jnp.where(
        lax.rem(at, PR) < PR // 2, mask_ref[0].astype(f32), mask_ref[1].astype(f32)
    )
    act[...] = (keep * positive * positive).astype(bf16)
    pos2[...] = keep * 2.0 * positive
    actcat[:, pl.ds(wrow, FD)] = act[pl.ds(pl.multiple_of(rows_c, FD), FD), :]
    ax = Remote(mate)
    ax.go(act.at[pl.ds(orow, FD)], actcat.at[:, pl.ds(wrow, FD)])
    act_float = act[...].astype(f32)
    norm_row = norms[0:1, :]
    lossb[0] = fold(act_float * norm_row) * penalty_weight
    wd.wait(wcat.at[pl.ds(orow, FD)])
    ax.wait(actcat.at[:, pl.ds(orow, FD)])

    def cols(xx, k):
        return pl.ds(pl.multiple_of(xx * SL + k * CW, CW), CW)

    def decode(xx, k):
        return jnp.dot(actcat[...], wcat[:, cols(xx, k)], preferred_element_type=f32)

    lo, hi = pl.ds(0, HALF), pl.ds(HALF, HALF)

    def reduce(k):
        o_r, o_l = Remote(right), Remote(left)
        d_r, d_l = Remote(right), Remote(left)
        a_r, a_l = Remote(right), Remote(left)
        part[:, cols(xo, k)] = decode(xo, k).astype(bf16)
        o_r.go(part.at[lo, cols(xo, k)], opl.at[k])
        o_l.go(part.at[hi, cols(xo, k)], opr.at[k])
        part[:, cols(xr, k)] = decode(xr, k).astype(bf16)
        d_r.go(part.at[hi, cols(xr, k)], inl.at[k, hi])
        part[:, cols(xl, k)] = decode(xl, k).astype(bf16)
        d_l.go(part.at[lo, cols(xl, k)], inr.at[k, lo])
        own[k] = decode(x, k)
        yield
        o_r.wait(opl.at[k])
        accr[k] = (part[lo, cols(xr, k)].astype(f32) + opl[k].astype(f32)).astype(bf16)
        a_r.go(accr.at[k], inl.at[k, lo])
        o_l.wait(opr.at[k])
        accl[k] = (part[hi, cols(xl, k)].astype(f32) + opr[k].astype(f32)).astype(bf16)
        a_l.go(accl.at[k], inr.at[k, hi])
        yield
        d_r.wait(inl.at[k, hi])
        d_l.wait(inr.at[k, lo])
        a_r.wait(inl.at[k, lo])
        a_l.wait(inr.at[k, hi])
        total = own[k] + inl[k].astype(f32) + inr[k].astype(f32)
        ssum[k] = total
        sumb[k] = total.astype(bf16)

        def zrows(zz):
            return pl.ds(pl.multiple_of(zz * PR, PR), PR)

        zbr = [None] + [Remote(dev(zz=zpeers[d])) for d in (1, 2, 3)]
        zar = [None] + [Remote(dev(zz=zpeers[d])) for d in (1, 2, 3)]
        zcr = Remote(dev(zz=zx))
        for d in (2, 1, 3):
            zbr[d].go(sumb.at[k, zrows(lax.rem(zpeers[d] + 4, NZ))], zb.at[k, d - 1])
        for d in (2, 1, 3):
            zar[d].go(sumb.at[k, zrows(zpeers[d])], za.at[k, d - 1])
        yield
        for d in (1, 2, 3):
            zbr[d].wait(zb.at[k, d - 1])
        relay = ssum[k, zrows(zx)]
        for d in range(3):
            relay = relay + zb[k, d].astype(f32)
        zr[k] = relay.astype(bf16)
        zcr.go(zr.at[k], zc.at[k])
        yield
        for d in (1, 2, 3):
            zar[d].wait(za.at[k, d - 1])
        recon = ssum[k, zrows(z)]
        for d in range(3):
            recon = recon + za[k, d].astype(f32)
        zcr.wait(zc.at[k])
        recon = recon + zc[k].astype(f32)
        there = pl.ds(k * CW, CW)
        misfit = recon - tfin[:, there].astype(f32)
        bk[pl.ds(pl.multiple_of(rows_c + z * PR, PR), PR), cols(x, k)] = misfit.astype(bf16)
        lossb[0] = lossb[0] + fold(misfit * misfit) * 0.5

    def whole(k):
        yield from reduce(k)
        yield from gather(bk, k)

    pipes = [whole(k) for k in range(CHUNKS)]
    step(*pipes)

    for q in range(0, D // 2, 512):
        gt[q : q + 512, :] = g[:, q : q + 512].T
    step(*pipes)
    for q in range(D // 2, D, 512):
        gt[q : q + 512, :] = g[:, q : q + 512].T
    act_t = act[...].T
    act_sum = jnp.sum(act_t.astype(f32), axis=1, keepdims=True)
    coef = penalty_weight * act_sum / norm_col
    step(*pipes)

    @pl.when(edge)
    def _():
        swap2.wait(tsw.at[1])
        tfin[...] = tsw[1]
        for r, s, dst in ((swap1, tsh, tsw.at[0]), (swap2, tsw.at[0], tsw.at[1])):
            pltpu.make_async_remote_copy(
                s, dst, send.at[r.i], recv.at[r.i],
                device_id=r.device, device_id_type=pl.DeviceIdType.MESH,
            ).wait_send()

    @pl.when(y < NY - 1)
    def _():
        tfin[...] = tsh[...]

    step(*pipes)
    step(*pipes)

    def total_loss():
        par = lax.rem(zphys // 4, 2)
        cur = lossb[0]
        stages = [
            mate,
            dev(xx=x + 1 - 2 * lax.rem(x, 2)),
            dev(xx=3 - x),
            dev(zh * NY + y + 1 - 2 * lax.rem(y, 2)),
            dev(zh * NY + 3 - y),
            None,
            far(4 + 8 * par),
            far(12 - 8 * par),
        ]
        for i, device in enumerate(stages):
            if device is None:
                lz[zq] = cur
                group = [None] + [Remote(dev(zz=zpeers[d])) for d in (1, 2, 3)]
                for d in (1, 2, 3):
                    group[d].go(lz.at[zq], lz.at[zq])
                yield
                for d in (1, 2, 3):
                    group[d].wait(lz.at[lax.rem(zq + 4 - d, 4)])
                cur = (lz[0] + lz[1]) + (lz[2] + lz[3])
            else:
                r = Remote(device)
                lsend[i] = cur
                r.go(lsend.at[i], lrecv.at[i])
                yield
                r.wait(lrecv.at[i])
                cur = cur + lrecv[i]
        loss_out[0, 0] = jnp.sum(cur) * scale

    loss_steps = total_loss()
    outs = []

    def backward(k):
        for xx in range(NX):
            at = xx * SL + k * CW
            back = bk[:, at : at + CW]
            w = wcat[pl.ds(wrow, FD), at : at + CW]
            grad = jnp.dot(act_t, back, preferred_element_type=f32)
            decb[:, at : at + CW] = (grad + coef * w.astype(f32)).astype(bf16)
            more = contract_last(back, w)
            if k == 0 and xx == 0:
                actg[...] = more
            else:
                actg[...] += more
            out = pltpu.make_async_copy(
                decb.at[:, pl.ds(at, CW)], dec_out.at[0, :, pl.ds(at, CW)],
                local.at[4 + k * NX + xx],
            )
            out.start()
            outs.append(out)

    for _ in range(6):
        step(*pipes)
        step(loss_steps)
    for k in range(CHUNKS):
        step(pipes[k])
        backward(k)
        step(loss_steps)

    pre_grad = ((actg[...] + penalty_weight * norm_row) * pos2[...]).astype(bf16)
    bias_out[...] = jnp.sum(pre_grad.astype(f32), axis=0, keepdims=True)
    for q in range(0, D, 512):
        grad = jnp.dot(gt[q : q + 512, :], pre_grad, preferred_element_type=f32)
        encb[q : q + 512, :] = grad.astype(bf16)
        out = pltpu.make_async_copy(
            encb.at[pl.ds(q, 512)], enc_out.at[0, pl.ds(q, 512)],
            local.at[4 + CHUNKS * NX + q // 512],
        )
        out.start()
        outs.append(out)
    for _ in range(10):
        step(loss_steps)
    for gen in (*gathers, *pipes, loss_steps):
        assert next(gen, "end") == "end"
    for d in sends:
        d.wait_send()
    for out in outs:
        out.wait()
    assert used[0] <= COPIES


def body(residual, targets, w_enc, b_enc, w_dec, block_mask):
    scale = 1.0 / (lax.axis_size("layer") * TOKENS * D)
    hbm = pl.BlockSpec(memory_space=pl.ANY)
    vmem = pl.BlockSpec(memory_space=pltpu.VMEM)
    smem = pl.BlockSpec(memory_space=pltpu.SMEM)
    enc_grad, bias_grad, dec_grad, loss = pl.pallas_call(
        lambda *refs: kernel(scale, *refs),
        name="transcoder_step",
        out_shape=(
            jax.ShapeDtypeStruct((1, D, FD), bf16),
            jax.ShapeDtypeStruct((1, FD), f32),
            jax.ShapeDtypeStruct((1, FD, D), bf16),
            jax.ShapeDtypeStruct((1, 1), f32),
        ),
        in_specs=[smem, hbm, hbm, hbm, vmem, hbm],
        out_specs=(hbm, vmem, hbm, smem),
        scratch_shapes=[
            pltpu.VMEM((NX, 4, SL), bf16),
            pltpu.VMEM((NX, 4, SL), bf16),
            pltpu.VMEM((PR, SL), bf16),
            pltpu.VMEM((PR, SL), bf16),
            pltpu.VMEM((2, PR, SL), bf16),
            pltpu.VMEM((PR, SL), bf16),
            pltpu.VMEM((TOKENS, D), bf16),
            pltpu.VMEM((D, TOKENS), bf16),
            pltpu.VMEM((TOKENS, D), bf16),
            pltpu.VMEM((D, FD), bf16),
            pltpu.VMEM((NC * FD, D), bf16),
            pltpu.VMEM((TOKENS, FD), bf16),
            pltpu.VMEM((CORE_ROWS, NC * FD), bf16),
            pltpu.VMEM((TOKENS, FD), f32),
            pltpu.VMEM((CORE_ROWS, D), bf16),
            pltpu.VMEM((CHUNKS, CORE_ROWS, CW), f32),
            pltpu.VMEM((CHUNKS, HALF, CW), bf16),
            pltpu.VMEM((CHUNKS, HALF, CW), bf16),
            pltpu.VMEM((CHUNKS, HALF, CW), bf16),
            pltpu.VMEM((CHUNKS, HALF, CW), bf16),
            pltpu.VMEM((CHUNKS, CORE_ROWS, CW), bf16),
            pltpu.VMEM((CHUNKS, CORE_ROWS, CW), bf16),
            pltpu.VMEM((CHUNKS, CORE_ROWS, CW), bf16),
            pltpu.VMEM((CHUNKS, CORE_ROWS, CW), f32),
            pltpu.VMEM((CHUNKS, 3, PR, CW), bf16),
            pltpu.VMEM((CHUNKS, 3, PR, CW), bf16),
            pltpu.VMEM((CHUNKS, PR, CW), bf16),
            pltpu.VMEM((CHUNKS, PR, CW), bf16),
            pltpu.VMEM((1, 8, 128), f32),
            pltpu.VMEM((8, 8, 128), f32),
            pltpu.VMEM((8, 8, 128), f32),
            pltpu.VMEM((4, 8, 128), f32),
            pltpu.VMEM((FD, FD), f32),
            pltpu.VMEM((TOKENS, FD), f32),
            pltpu.VMEM((FD, D), bf16),
            pltpu.VMEM((D, FD), bf16),
            pltpu.SemaphoreType.DMA((COPIES,)),
            pltpu.SemaphoreType.DMA((COPIES,)),
            pltpu.SemaphoreType.DMA((32,)),
        ],
        compiler_params=pltpu.CompilerParams(
            collective_id=0, has_side_effects=True, vmem_limit_bytes=48 << 20
        ),
    )(block_mask.reshape(2), residual, targets, w_enc, b_enc, w_dec)
    return enc_grad, bias_grad, dec_grad, loss.reshape(())


def solution(mesh):
    return jax.shard_map(
        body,
        mesh=mesh,
        in_specs=(
            P("layer", "feat", None),
            P("layer", "feat", None),
            P("layer", None, "feat"),
            P("layer", "feat"),
            P("layer", "feat", None),
            P("layer", None, "feat"),
        ),
        out_specs=(P("layer", None, "feat"), P("layer", "feat"), P("layer", "feat", None), P()),
        check_vma=False,
    )
```

time: 1160 us -> 106 us (0.09)
  the two profiles are of different devices: /device:TPU:1 before, /device:TPU:8 now
where the time goes in v1:
time: 106 us; the launch traced here: 105 us
  Pallas kernels  95.8 us (90%)
  local copies, waits for them, and re-layouts  7.07 us (7%)
  between operations  2.48 us (2%)
    pallas_call x1, Pallas kernels, body(): pl.pallas_call(lambda *refs: kernel(scale, *refs), name='transcoder_step'...  95.8 us
    unnamed x15, local copies, waits for them, and re-layouts  7.07 us

profile of v1, /device:TPU:8, one launch (start us, length us, event | category | flops | bytes accessed | tf_op | source)
XLA Modules:
  0.0 105.4 jit_solution(4087640276631081843)
XLA Ops:
  0.6 0.0 copy-start.4
  0.6 0.0 copy-start.5
  0.7 0.6 copy-done.4
  1.3 0.0 copy-done.5
  1.3 0.0 copy-start
  1.3 1.2 %copy-done = bf16[1,4096,128]{2,1,0:T(8,128)(2,1)S(1)} copy-done((bf16[1,4096,128]{2,1,0:T(8,128)(2,1)S(1)}, bf16[1,4096,128]{2,1,0:T(8,128)(2,1)}, u32[]{:S(2)}) %copy-start) | copy-done | bytes 1048600
  2.5 0.0 copy-start.1
  2.5 1.2 %copy-done.1 = bf16[1,128,4096]{2,1,0:T(8,128)(2,1)S(1)} copy-done((bf16[1,128,4096]{2,1,0:T(8,128)(2,1)S(1)}, bf16[1,128,4096]{2,1,0:T(8,128)(2,1)}, u32[]{:S(2)}) %copy-start.1) | copy-done | bytes 1048600
  3.8 0.0 copy-start.2
  3.8 0.8 copy-done.2
  4.5 0.0 copy-start.3
  4.5 0.8 copy-done.3
  5.3 95.8 %transcoder_step.1 = (bf16[1,4096,128]{2,1,0:T(8,128)(2,1)S(1)}, f32[1,128]{1,0:T(1,128)S(1)}, bf16[1,128,4096]{2,1,0:T(8,128)(2,1)S(1)}, f32[1,1]{1,0:T(1,128)}) custom-call(s32[2]{0:T(128)S(1)} %bitcast.2, bf16[1,4,4096]{2,1,0:T(4,128)(2,1)S(1)} %copy-done.2, bf16[1,4,4096]{2,1,0:T(4,128)(2,1)S(1)} %copy-done.3, bf16[1,4096,128]{2,1,0:T(8,128)(2,1)S(1)} %copy-done, ...), custom_call_target="tpu_custom_call" | custom-call | tf_op jit(solution)/shard_map/transcoder_step/pallas_call | solution.py:460
  101.1 1.0 copy.14
  102.1 0.5 copy.15
  102.6 1.0 copy.16
Async XLA Ops:
  0.6 0.7 copy-start.4
  0.6 0.7 copy-start.5
  1.3 1.2 %copy-start = (bf16[1,4096,128]{2,1,0:T(8,128)(2,1)S(1)}, bf16[1,4096,128]{2,1,0:T(8,128)(2,1)}, u32[]{:S(2)}) copy-start(bf16[1,4096,128]{2,1,0:T(8,128)(2,1)} %refs_3_.1) | copy-start | bytes 3145732
  2.5 1.2 %copy-start.1 = (bf16[1,128,4096]{2,1,0:T(8,128)(2,1)S(1)}, bf16[1,128,4096]{2,1,0:T(8,128)(2,1)}, u32[]{:S(2)}) copy-start(bf16[1,128,4096]{2,1,0:T(8,128)(2,1)} %refs_5_.1) | copy-start | bytes 3145732
  3.8 0.8 copy-start.2
  4.5 0.8 copy-start.3

commit v2 on v1

v2 whole, which is shorter than its diff:
```python
import jax
import jax.numpy as jnp
from jax import lax
from jax.experimental import pallas as pl
from jax.experimental.pallas import tpu as pltpu
from jax.sharding import PartitionSpec as P

NX, NZ, NC, NY = 4, 8, 2, 4
TOKENS, D, FD = 256, 4096, 128
SL = D // NX
CORE_ROWS = TOKENS // NC
HALF = CORE_ROWS // 2
PR = CORE_ROWS // NZ
GCHUNKS = 2
GW = SL // GCHUNKS
CHUNKS = 2
CW = SL // CHUNKS
GROUPS = 55

penalty_weight = 0.5
norm_epsilon = 1e-06
f32, bf16 = jnp.float32, jnp.bfloat16


def contract_last(a, b):
    return lax.dot_general(a, b, (((1,), (1,)), ((), ())), preferred_element_type=f32)


def fold(v):
    total = None
    for r in range(0, v.shape[0], 8):
        for q in range(0, v.shape[1], 128):
            tile = v[r : r + 8, q : q + 128]
            total = tile if total is None else total + tile
    return total


def kernel(
    scale,
    mask_hbm, res_ref, tgt_ref, wenc_hbm, benc_hbm, wdec_hbm,
    enc_out, bias_out, dec_out, loss_out,
    mask, benc, raw, traw, tp, tsh, tsw, tfin, g, gt, bk, wenc, wcat, act, actcat, pos2,
    part, own, opl, opr, accr, accl, inl, inr, sumb, ssum, zab, zs, zc, lossb, lxc, lfar,
    lz, ly, norms, actg, send, recv, local,
):
    layer = lax.axis_index("layer")
    feat = lax.axis_index("feat")
    zh, y = layer // NY, lax.rem(layer, NY)
    c = lax.rem(feat, NC)
    z = lax.rem(feat // NC, NZ)
    x = feat // (NC * NZ)
    h, zq = z // 4, lax.rem(z, 4)
    xr, xo, xl = (lax.rem(x + d, NX) for d in (1, 2, 3))

    def dev(l=layer, xx=x, zz=z, cc=c):
        return (l, (xx * NZ + zz) * NC + cc)

    zpeers = [h * 4 + lax.rem(zq + d, 4) for d in range(4)]
    zfrom = [h * 4 + lax.rem(zq + 4 - d, 4) for d in range(4)]
    zx = lax.rem(z + 4, NZ)
    zphys = zh * NZ + z

    def far(step):
        zz = lax.rem(zphys + step, 2 * NZ)
        return dev((zz // NZ) * NY + y, x, lax.rem(zz, NZ))

    up, down = far(4), far(12)
    ys = [dev(zh * NY + lax.rem(y + d, NY)) for d in range(NY)]
    mate = dev(cc=1 - c)
    right, left, opp = dev(xx=xr), dev(xx=xl), dev(xx=xo)
    cross = dev(zz=zx)

    used = [0]
    sends = []

    class Group:
        def __init__(self, like, final=True):
            self.i, self.like = used[0], like
            used[0] += 1
            if final:
                sends.append(self)

        def copy(self, src, dst, device):
            return pltpu.make_async_remote_copy(
                src, dst, send.at[self.i], recv.at[self.i],
                device_id=device, device_id_type=pl.DeviceIdType.MESH,
            )

        def go(self, device, src, dst=None):
            self.copy(src, src if dst is None else dst, device).start()

        def wait(self):
            self.copy(self.like, self.like, mate).wait_recv()

        def sent(self):
            self.copy(self.like, self.like, mate).wait_send()

    wrow = pl.multiple_of(c * FD, FD)
    orow = pl.multiple_of((1 - c) * FD, FD)
    loads = [
        pltpu.make_async_copy(src, dst, local.at[i])
        for i, (src, dst) in enumerate((
            (wdec_hbm.at[0], wcat.at[pl.ds(wrow, FD)]), (wenc_hbm.at[0], wenc),
            (mask_hbm, mask), (benc_hbm, benc),
        ))
    ]
    for load in loads:
        load.start()

    barrier = pltpu.get_barrier_semaphore()
    partners = [
        mate, right, left, opp, *(dev(zz=q) for q in zpeers[1:]), up, down, *ys[1:],
        *(dev(xx=lax.rem(x + d, NX), cc=1 - c) for d in (1, 2, 3)),
    ]
    for p in partners:
        pl.semaphore_signal(barrier, inc=1, device_id=p, device_id_type=pl.DeviceIdType.MESH)
    pl.semaphore_wait(barrier, len(partners))

    rows_c = c * CORE_ROWS

    def slab(xx):
        return pl.ds(pl.multiple_of(xx * SL, SL), SL)

    def stage0(src, buf, sem):
        got = Group(buf.at[pl.ds(0, 3)])
        for device, xx in ((opp, xo), (right, xr), (left, xl)):
            got.go(device, src.at[0, :, slab(xx)], buf.at[x])
        mine = pltpu.make_async_copy(src.at[0, :, slab(x)], buf.at[x], local.at[sem])
        mine.start()

        def finish():
            mine.wait()
            got.wait()
            return jnp.concatenate([buf[i].astype(f32) for i in range(NX)], axis=0).astype(bf16)

        return finish

    res_done = stage0(res_ref, raw, 4)
    tgt_done = stage0(tgt_ref, traw, 5)

    def blocks(buf, k, cw):
        def rows(first, n, xx, at=0, width=cw):
            return buf.at[
                pl.ds(pl.multiple_of(first, 16), n),
                pl.ds(pl.multiple_of(xx * SL + k * cw + at, 128), width),
            ]

        return rows

    def gather(buf, k, cw):
        rows = blocks(buf, k, cw)

        def like(n, width=cw):
            return buf.at[pl.ds(0, n), pl.ds(0, width)]

        def piece(zz):
            return rows(rows_c + zz * PR, PR, x)

        def half(hh, xx):
            return rows(rows_c + hh * HALF, HALF, xx)

        def side(hh, s, xx):
            return rows(rows_c + hh * HALF, HALF, xx, s * (cw // 2), cw // 2)

        z1, zcr, z2 = Group(like(3 * PR)), Group(like(PR)), Group(like(3 * PR))
        xrt = [Group(like(HALF)) for _ in range(2)]
        xlt = [Group(like(HALF)) for _ in range(2)]
        fwd = [Group(like(HALF)) for _ in range(2)]
        mates = Group(like(CORE_ROWS, NX * cw))
        o = 1 - h

        def ring(i, zz):
            xrt[i].go(right, piece(zz))
            xlt[i].go(left, piece(zz))

        zcr.go(cross, piece(z))
        for d in (2, 1, 3):
            z1.go(dev(zz=zpeers[d]), piece(z))
        ring(0, z)
        yield
        z1.wait()
        for d in (1, 3, 2):
            ring(0, zfrom[d])
        mates.go(mate, half(h, x))
        yield
        zcr.wait()
        for d in (2, 1, 3):
            z2.go(dev(zz=zpeers[d]), piece(zx))
        ring(1, zx)
        yield
        z2.wait()
        for d in (1, 3, 2):
            ring(1, lax.rem(zfrom[d] + 4, NZ))
        mates.go(mate, half(o, x))
        for i, hh in enumerate((h, o)):
            yield
            xrt[i].wait()
            fwd[i].go(right, side(hh, 0, xl))
            mates.go(mate, half(hh, xl))
            xlt[i].wait()
            fwd[i].go(left, side(hh, 1, xr))
            mates.go(mate, half(hh, xr))
        yield
        for i, hh in enumerate((h, o)):
            fwd[i].wait()
            mates.go(mate, half(hh, xo))
        yield
        mates.wait()

    def gather2(buf, k, cw):
        rows = blocks(buf, k, cw)

        def like(n, width=cw):
            return buf.at[pl.ds(0, n), pl.ds(0, width)]

        def piece(zz):
            return rows(rows_c + zz * PR, PR, x)

        def all_of(xx, at=0, width=cw):
            return rows(rows_c, CORE_ROWS, xx, at, width)

        z1 = Group(like(6 * PR))
        xrt, xlt = Group(like(CORE_ROWS)), Group(like(CORE_ROWS))
        fwd = Group(like(CORE_ROWS))
        mates = Group(like(CORE_ROWS, NX * cw))

        def ring(zz):
            xrt.go(right, piece(zz))
            xlt.go(left, piece(zz))

        both = (zq, zq + 4)
        for d in (2, 1, 3):
            for zz in both:
                z1.go(dev(zz=zpeers[d]), piece(zz))
        for zz in both:
            ring(zz)
        yield
        z1.wait()
        for d in (1, 3, 2):
            for zz in (lax.rem(zfrom[d], 4), lax.rem(zfrom[d], 4) + 4):
                ring(zz)
        mates.go(mate, all_of(x))
        yield
        xrt.wait()
        fwd.go(right, all_of(xl, 0, cw // 2))
        xlt.wait()
        fwd.go(left, all_of(xr, cw // 2, cw // 2))
        mates.go(mate, all_of(xl))
        mates.go(mate, all_of(xr))
        yield
        fwd.wait()
        mates.go(mate, all_of(xo))
        yield
        mates.wait()

    loads[0].wait()
    wd = Group(wcat.at[pl.ds(wrow, FD)])
    wd.go(mate, wcat.at[pl.ds(wrow, FD)])

    first = res_done()
    g[pl.ds(pl.multiple_of(rows_c + z * PR, PR), PR), slab(x)] = first
    gathers = [gather(g, k, GW) for k in range(GCHUNKS)]

    def step(*gens):
        for gen in gens:
            next(gen, None)

    step(*gathers)

    tp[...] = tgt_done()
    shift = Group(tsh)
    shift.go(ys[3], tp, tsh)

    sq = jnp.zeros((FD, 128), f32)
    for q in range(0, D, 512):
        w = wcat[pl.ds(wrow, FD), q : q + 512].astype(f32)
        w = w * w
        sq = sq + (w[:, :128] + w[:, 128:256]) + (w[:, 256:384] + w[:, 384:])
    norm_col = jnp.sqrt(jnp.sum(sq, axis=1, keepdims=True) + norm_epsilon)
    norms[...] = jnp.broadcast_to(norm_col, (FD, FD)).T

    step(*gathers)
    step(*gathers)

    shift.wait()
    swap1, swap2 = Group(tsw.at[0], False), Group(tsw.at[1], False)
    edge = y == NY - 1

    @pl.when(edge)
    def _():
        swap1.go(up, tsh, tsw.at[0])

    for _ in range(3):
        step(*gathers)

    @pl.when(edge)
    def _():
        swap1.wait()
        swap2.go(up, tsw.at[0], tsw.at[1])

    for _ in range(2):
        step(*gathers)

    loads[1].wait()
    loads[2].wait()
    loads[3].wait()
    pre = jnp.dot(g[...], wenc[...], preferred_element_type=f32) + benc[...]
    positive = jnp.maximum(pre, 0.0)
    at = lax.broadcasted_iota(jnp.int32, (TOKENS, FD), 0)
    keep = jnp.where(lax.rem(at, PR) < PR // 2, mask[0].astype(f32), mask[1].astype(f32))
    act[...] = (keep * positive * positive).astype(bf16)
    pos2[...] = keep * 2.0 * positive
    ax = Group(actcat.at[:, pl.ds(0, FD)])
    ax.go(mate, act.at[pl.ds(orow, FD)], actcat.at[:, pl.ds(wrow, FD)])
    actcat[:, pl.ds(wrow, FD)] = act[pl.ds(pl.multiple_of(rows_c, FD), FD), :]
    norm_row = norms[0:1, :]
    lossb[0] = fold(act[...].astype(f32) * norm_row) * penalty_weight

    @pl.when(edge)
    def _():
        swap2.wait()
        tfin[h] = tsw[1]
        swap1.sent()
        swap2.sent()

    @pl.when(y < NY - 1)
    def _():
        tfin[h] = tsh[...]

    tx = Group(tfin.at[0])
    tx.go(cross, tfin.at[h], tfin.at[h])
    wd.wait()
    ax.wait()

    def cols(xx, k):
        return pl.ds(pl.multiple_of(xx * SL + k * CW, CW), CW)

    def decode(xx, k):
        return jnp.dot(actcat[...], wcat[:, cols(xx, k)], preferred_element_type=f32)

    lo, hi = pl.ds(0, HALF), pl.ds(HALF, HALF)

    def zrows(zz):
        return pl.ds(pl.multiple_of(zz * PR, PR), PR)

    def reduce(k):
        o_r, o_l, direct, summed = (
            Group(opl.at[k]), Group(opr.at[k]), Group(inl.at[k]), Group(inl.at[k])
        )
        part[:, cols(xo, k)] = decode(xo, k).astype(bf16)
        o_r.go(right, part.at[lo, cols(xo, k)], opl.at[k])
        o_l.go(left, part.at[hi, cols(xo, k)], opr.at[k])
        part[:, cols(xr, k)] = decode(xr, k).astype(bf16)
        direct.go(right, part.at[hi, cols(xr, k)], inl.at[k, hi])
        part[:, cols(xl, k)] = decode(xl, k).astype(bf16)
        direct.go(left, part.at[lo, cols(xl, k)], inr.at[k, lo])
        own[k] = decode(x, k)
        yield
        o_r.wait()
        accr[k] = (part[lo, cols(xr, k)].astype(f32) + opl[k].astype(f32)).astype(bf16)
        summed.go(right, accr.at[k], inl.at[k, lo])
        o_l.wait()
        accl[k] = (part[hi, cols(xl, k)].astype(f32) + opr[k].astype(f32)).astype(bf16)
        summed.go(left, accl.at[k], inr.at[k, hi])
        yield
        direct.wait()
        summed.wait()
        total = own[k] + inl[k].astype(f32) + inr[k].astype(f32)
        ssum[k] = total
        sumb[k] = total.astype(bf16)
        near = Group(zab.at[k])
        for d in (2, 1, 3):
            for hh in range(2):
                near.go(
                    dev(zz=zpeers[d]),
                    sumb.at[k, zrows(lax.rem(zpeers[d], 4) + 4 * hh)],
                    zab.at[k, d - 1, hh],
                )
        yield
        near.wait()
        for hh in range(2):
            part_sum = ssum[k, zrows(zq + 4 * hh)]
            for d in range(3):
                part_sum = part_sum + zab[k, d, hh].astype(f32)
            zs[k, hh] = part_sum.astype(bf16)
        over = Group(zc.at[k])
        over.go(cross, zs.at[k], zc.at[k])
        yield
        over.wait()
        if k == 0:
            tx.wait()
        for hh in range(2):
            recon = zs[k, hh].astype(f32) + zc[k, hh].astype(f32)
            misfit = recon - tfin[hh, :, k * CW : (k + 1) * CW].astype(f32)
            bk[pl.ds(pl.multiple_of(rows_c + (zq + 4 * hh) * PR, PR), PR), cols(x, k)] = (
                misfit.astype(bf16)
            )
            mine = (h == hh).astype(f32) * 0.5
            lossb[0] = lossb[0] + fold(misfit * misfit) * mine

    def total_loss():
        par = lax.rem(zphys // 4, 2)
        xc = x * NC + c
        s1 = Group(lxc.at[pl.ds(0, 7)])
        lxc[xc] = lossb[0]
        for d in range(NX):
            for e in range(NC):
                if d or e:
                    device = dev(xx=lax.rem(x + d, NX), cc=c if not e else 1 - c)
                    s1.go(device, lxc.at[xc])
        yield
        s1.wait()
        cur = lxc[0]
        for i in range(1, NX * NC):
            cur = cur + lxc[i]
        for i, device in enumerate((far(4 + 8 * par), far(12 - 8 * par))):
            s2 = Group(lfar.at[2 * i])
            lfar[2 * i] = cur
            s2.go(device, lfar.at[2 * i], lfar.at[2 * i + 1])
            yield
            s2.wait()
            cur = cur + lfar[2 * i + 1]
        s3 = Group(lz.at[pl.ds(0, 3)])
        lz[zq] = cur
        for d in (1, 2, 3):
            s3.go(dev(zz=zpeers[d]), lz.at[zq])
        yield
        s3.wait()
        cur = (lz[0] + lz[1]) + (lz[2] + lz[3])
        s4 = Group(ly.at[pl.ds(0, 3)])
        ly[y] = cur
        for d in (1, 2, 3):
            s4.go(ys[d], ly.at[y])
        yield
        s4.wait()
        cur = (ly[0] + ly[1]) + (ly[2] + ly[3])
        loss_out[0, 0] = jnp.sum(cur) * scale

    loss_steps = total_loss()

    def whole(k):
        yield from reduce(k)
        if k == CHUNKS - 1:
            step(loss_steps)
        yield from gather2(bk, k, CW)

    pipes = [whole(k) for k in range(CHUNKS)]
    step(*pipes)

    for q in range(0, D // 2, 512):
        gt[q : q + 512, :] = g[:, q : q + 512].T
    step(*pipes)
    for q in range(D // 2, D, 512):
        gt[q : q + 512, :] = g[:, q : q + 512].T
    act_t = act[...].T
    act_sum = jnp.sum(act_t.astype(f32), axis=1, keepdims=True)
    coef = penalty_weight * act_sum / norm_col
    for _ in range(3):
        step(*pipes)

    def backward(k):
        for xx in range(NX):
            at = xx * SL + k * CW
            back = bk[:, at : at + CW]
            w = wcat[pl.ds(wrow, FD), at : at + CW]
            grad = jnp.dot(act_t, back, preferred_element_type=f32)
            dec_out[0, :, at : at + CW] = (grad + coef * w.astype(f32)).astype(bf16)
            more = contract_last(back, w)
            if k == 0 and xx == 0:
                actg[...] = more
            else:
                actg[...] += more

    step(loss_steps)
    step(*pipes)
    step(loss_steps)
    step(*pipes)
    step(*pipes)
    step(loss_steps)
    for k in range(CHUNKS):
        step(pipes[k])
        backward(k)

    pre_grad = ((actg[...] + penalty_weight * norm_row) * pos2[...]).astype(bf16)
    bias_out[...] = jnp.sum(pre_grad.astype(f32), axis=0, keepdims=True)
    for q in range(0, D, 512):
        grad = jnp.dot(gt[q : q + 512, :], pre_grad, preferred_element_type=f32)
        enc_out[0, q : q + 512, :] = grad.astype(bf16)
    step(loss_steps)
    step(loss_steps)
    for gen in (*gathers, *pipes, loss_steps):
        assert next(gen, "end") == "end"
    for group in sends:
        group.sent()
    assert used[0] == GROUPS, used[0]


def write_out(*refs):
    copies = [
        pltpu.make_async_copy(src, dst, refs[8].at[i])
        for i, (src, dst) in enumerate(zip(refs[:4], refs[4:8]))
    ]
    for copy in copies:
        copy.start()
    for copy in copies:
        copy.wait()


def body(residual, targets, w_enc, b_enc, w_dec, block_mask):
    scale = 1.0 / (lax.axis_size("layer") * TOKENS * D)
    hbm = pl.BlockSpec(memory_space=pltpu.HBM)
    vmem = pl.BlockSpec(memory_space=pltpu.VMEM)
    smem = pl.BlockSpec(memory_space=pltpu.SMEM)
    enc_grad, bias_grad, dec_grad, loss = pl.pallas_call(
        lambda *refs: kernel(scale, *refs),
        name="transcoder_step",
        out_shape=(
            jax.ShapeDtypeStruct((1, D, FD), bf16),
            jax.ShapeDtypeStruct((1, FD), f32),
            jax.ShapeDtypeStruct((1, FD, D), bf16),
            jax.ShapeDtypeStruct((1, 1), f32),
        ),
        in_specs=[hbm] * 6,
        out_specs=(vmem, vmem, vmem, smem),
        scratch_shapes=[
            pltpu.SMEM((2,), jnp.int32),
            pltpu.VMEM((1, FD), f32),
            pltpu.VMEM((NX, 4, SL), bf16),
            pltpu.VMEM((NX, 4, SL), bf16),
            pltpu.VMEM((PR, SL), bf16),
            pltpu.VMEM((PR, SL), bf16),
            pltpu.VMEM((2, PR, SL), bf16),
            pltpu.VMEM((2, PR, SL), bf16),
            pltpu.VMEM((TOKENS, D), bf16),
            pltpu.VMEM((D, TOKENS), bf16),
            pltpu.VMEM((TOKENS, D), bf16),
            pltpu.VMEM((D, FD), bf16),
            pltpu.VMEM((NC * FD, D), bf16),
            pltpu.VMEM((TOKENS, FD), bf16),
            pltpu.VMEM((CORE_ROWS, NC * FD), bf16),
            pltpu.VMEM((TOKENS, FD), f32),
            pltpu.VMEM((CORE_ROWS, D), bf16),
            pltpu.VMEM((CHUNKS, CORE_ROWS, CW), f32),
            pltpu.VMEM((CHUNKS, HALF, CW), bf16),
            pltpu.VMEM((CHUNKS, HALF, CW), bf16),
            pltpu.VMEM((CHUNKS, HALF, CW), bf16),
            pltpu.VMEM((CHUNKS, HALF, CW), bf16),
            pltpu.VMEM((CHUNKS, CORE_ROWS, CW), bf16),
            pltpu.VMEM((CHUNKS, CORE_ROWS, CW), bf16),
            pltpu.VMEM((CHUNKS, CORE_ROWS, CW), bf16),
            pltpu.VMEM((CHUNKS, CORE_ROWS, CW), f32),
            pltpu.VMEM((CHUNKS, 3, 2, PR, CW), bf16),
            pltpu.VMEM((CHUNKS, 2, PR, CW), bf16),
            pltpu.VMEM((CHUNKS, 2, PR, CW), bf16),
            pltpu.VMEM((1, 8, 128), f32),
            pltpu.VMEM((NX * NC, 8, 128), f32),
            pltpu.VMEM((4, 8, 128), f32),
            pltpu.VMEM((4, 8, 128), f32),
            pltpu.VMEM((NY, 8, 128), f32),
            pltpu.VMEM((FD, FD), f32),
            pltpu.VMEM((TOKENS, FD), f32),
            pltpu.SemaphoreType.DMA((GROUPS,)),
            pltpu.SemaphoreType.DMA((GROUPS,)),
            pltpu.SemaphoreType.DMA((6,)),
        ],
        compiler_params=pltpu.CompilerParams(
            collective_id=0, has_side_effects=True, vmem_limit_bytes=48 << 20
        ),
    )(*(pltpu.with_memory_space_constraint(a, pltpu.HBM) for a in (block_mask.reshape(2), residual, targets, w_enc, b_enc, w_dec)))
    results = (enc_grad, bias_grad, dec_grad, loss)
    enc_grad, bias_grad, dec_grad, loss = pl.pallas_call(
        write_out,
        name="write_out",
        out_shape=tuple(jax.ShapeDtypeStruct(r.shape, r.dtype) for r in results),
        in_specs=[pl.BlockSpec(memory_space=pl.ANY)] * 4,
        out_specs=(hbm,) * 4,
        scratch_shapes=[pltpu.SemaphoreType.DMA((4,))],
        compiler_params=pltpu.CompilerParams(vmem_limit_bytes=16 << 20),
    )(*results)
    return enc_grad, bias_grad, dec_grad, loss.reshape(())


def solution(mesh):
    return jax.shard_map(
        body,
        mesh=mesh,
        in_specs=(
            P("layer", "feat", None),
            P("layer", "feat", None),
            P("layer", None, "feat"),
            P("layer", "feat"),
            P("layer", "feat", None),
            P("layer", None, "feat"),
        ),
        out_specs=(P("layer", None, "feat"), P("layer", "feat"), P("layer", "feat", None), P()),
        check_vma=False,
    )
```

time: 106 us -> 85.4 us (0.81)
  the two profiles are of different devices: /device:TPU:8 before, /device:TPU:1 now
where the time goes in v2:
time: 85.4 us; the launch traced here: 84.4 us
  Pallas kernels  83.8 us (98%)
    pallas_call x1, Pallas kernels, body(): pl.pallas_call(lambda *refs: kernel(scale, *refs), name='transcoder_step'...  81.8 us
    pallas_call x1, Pallas kernels, body(): pl.pallas_call(write_out, name='write_out', out_shape=tuple((jax.ShapeDty...  1.99 us

profile of v2, /device:TPU:1, one launch (start us, length us, event | category | flops | bytes accessed | tf_op | source)
XLA Modules:
  0.0 84.4 jit_solution(7426726682549050083)
XLA Ops:
  0.6 81.8 %transcoder_step.1 = (bf16[1,4096,128]{2,1,0:T(8,128)(2,1)S(1)}, f32[1,128]{1,0:T(1,128)S(1)}, bf16[1,128,4096]{2,1,0:T(8,128)(2,1)S(1)}, f32[1,1]{1,0:T(1,128)}) custom-call(s32[2]{0:T(128)} %bitcast.2, bf16[1,4,4096]{2,1,0:T(4,128)(2,1)} %refs_1_.1, bf16[1,4,4096]{2,1,0:T(4,128)(2,1)} %refs_2_.1, bf16[1,4096,128]{2,1,0:T(8,128)(2,1)} %refs_3_.1, ...), custom_call_target="tpu_custom_call" | custom-call | tf_op jit(solution)/shard_map/transcoder_step/pallas_call | solution.py:514
  82.4 2.0 %write_out.1 = (bf16[1,4096,128]{2,1,0:T(8,128)(2,1)}, f32[1,128]{1,0:T(1,128)}, bf16[1,128,4096]{2,1,0:T(8,128)(2,1)}, f32[1,1]{1,0:T(1,128)}) custom-call(bf16[1,4096,128]{2,1,0:T(8,128)(2,1)S(1)} %get-tuple-element.12.refs_0_, f32[1,128]{1,0:T(1,128)S(1)} %get-tuple-element.13.refs_1_, bf16[1,128,4096]{2,1,0:T(8,128)(2,1)S(1)} %get-tuple-element.14.refs_2_, ...), custom_call_target="tpu_custom_call" | custom-call | tf_op jit(solution)/shard_map/write_out/pallas_call | solution.py:571

commit v3 on v2

v3 whole, which is shorter than its diff:
```python
import math

import jax
import jax.numpy as jnp
from jax import lax
from jax.experimental import pallas as pl
from jax.experimental.pallas import tpu as pltpu
from jax.sharding import PartitionSpec as P

NX, NZ, NC, NY = 4, 8, 2, 4
TOKENS, D, FD = 256, 4096, 128
SL = D // NX
CORE_ROWS = TOKENS // NC
HALF = CORE_ROWS // 2
PR = CORE_ROWS // NZ
GCHUNKS = 2
GW = SL // GCHUNKS
CHUNKS = 2
CW = SL // CHUNKS
GROUPS = 86
POOLS = 11
SPLIT = 1
POOL = 1 << 20

penalty_weight = 0.5
norm_epsilon = 1e-06
f32, bf16 = jnp.float32, jnp.bfloat16


def contract_last(a, b):
    return lax.dot_general(a, b, (((1,), (1,)), ((), ())), preferred_element_type=f32)


def fold(v):
    total = None
    for r in range(0, v.shape[0], 8):
        for q in range(0, v.shape[1], 128):
            tile = v[r : r + 8, q : q + 128]
            total = tile if total is None else total + tile
    return total


def kernel(
    scale,
    mask_hbm, res_ref, tgt_ref, wenc_hbm, benc_hbm, wdec_hbm,
    enc_out, bias_out, dec_out, loss_out,
    mask, bcat, mk, resv, tgtv, raw, traw, tp, tsh, tsw, tfin, g, gt, bk, wencc, wcat, act, actcat,
    pos2, p2cat, part, own, opl, opr, accr, accl, inl, inr, sumb, ssum, za, zs, zc, lossb, lxc, lfar,
    lz, ly, norms, actg, send, recv, local,
):
    layer = lax.axis_index("layer")
    feat = lax.axis_index("feat")
    zh, y = layer // NY, lax.rem(layer, NY)
    c = lax.rem(feat, NC)
    z = lax.rem(feat // NC, NZ)
    x = feat // (NC * NZ)
    h, zq = z // 4, lax.rem(z, 4)
    xr, xo, xl = (lax.rem(x + d, NX) for d in (1, 2, 3))

    def dev(l=layer, xx=x, zz=z, cc=c):
        return (l, (xx * NZ + zz) * NC + cc)

    near_q = [zq + 1 - 2 * lax.rem(zq, 2), lax.rem(zq + 2, 4), 3 - zq]
    near_z = [h * 4 + q for q in near_q]
    near_dev = [dev(zz=zz) for zz in near_z]
    zx = lax.rem(z + 4, NZ)
    zphys = zh * NZ + z

    def far(step):
        zz = lax.rem(zphys + step, 2 * NZ)
        return dev((zz // NZ) * NY + y, x, lax.rem(zz, NZ))

    up, down = far(4), far(12)
    ys = [dev(zh * NY + lax.rem(y + d, NY)) for d in range(NY)]
    mate = dev(cc=1 - c)
    right, left, opp = dev(xx=xr), dev(xx=xl), dev(xx=xo)
    cross = dev(zz=zx)

    used = [0]
    pools = []

    class Group:
        def __init__(self, like, kind="main"):
            self.i, self.like = used[0], like
            used[0] += 1
            size = math.prod(like.shape) * jnp.dtype(like.dtype).itemsize
            for p, (other, total) in enumerate(pools):
                if other == kind and total + size <= POOL:
                    self.pool = p
                    pools[p] = (kind, total + size)
                    break
            else:
                self.pool = len(pools)
                pools.append((kind, size))

        def copy(self, src, dst, device):
            return pltpu.make_async_remote_copy(
                src, dst, send.at[self.pool], recv.at[self.i],
                device_id=device, device_id_type=pl.DeviceIdType.MESH,
            )

        def go(self, device, src, dst=None):
            self.copy(src, src if dst is None else dst, device).start()

        def wait(self):
            self.copy(self.like, self.like, mate).wait_recv()

    def sent(kinds):
        for p, (kind, total) in enumerate(pools):
            if kind in kinds:
                if total % 8192 == 0:
                    like = gt.at[pl.ds(0, total // 512), :]
                elif total % 4096 == 0:
                    like = gt.at[pl.ds(0, total // 256), pl.ds(0, 128)]
                else:
                    like = bcat.at[:, pl.ds(0, total // 4)]
                pltpu.make_async_remote_copy(
                    like, like, send.at[p], recv.at[0],
                    device_id=mate, device_id_type=pl.DeviceIdType.MESH,
                ).wait_send()

    wrow = pl.multiple_of(c * FD, FD)
    orow = pl.multiple_of((1 - c) * FD, FD)
    loads = [
        pltpu.make_async_copy(src, dst, local.at[i])
        for i, (src, dst) in enumerate((
            (wdec_hbm.at[0], wcat.at[pl.ds(wrow, FD)]),
            (wenc_hbm.at[0], wencc.at[:, pl.ds(wrow, FD)]),
            (mask_hbm, mask), (benc_hbm, bcat.at[:, pl.ds(wrow, FD)]),
            (res_ref, resv), (tgt_ref, tgtv),
        ))
    ]
    for load in (loads[4], loads[5], *loads[:4]):
        load.start()

    barrier = pltpu.get_barrier_semaphore()
    partners = [
        mate, right, left, opp, *near_dev, up, down, *ys[1:],
        *(dev(xx=lax.rem(x + d, NX), cc=1 - c) for d in (1, 2, 3)),
    ]
    for p in partners:
        pl.semaphore_signal(barrier, inc=1, device_id=p, device_id_type=pl.DeviceIdType.MESH)
    pl.semaphore_wait(barrier, len(partners))

    rows_c = c * CORE_ROWS

    def slab(xx):
        return pl.ds(pl.multiple_of(xx * SL, SL), SL)

    def stage0(src, buf, sem):
        got = Group(buf.at[pl.ds(0, 3)])
        for device, xx in ((opp, xo), (right, xr), (left, xl)):
            got.go(device, src.at[0, :, slab(xx)], buf.at[x])
        mine = pltpu.make_async_copy(src.at[0, :, slab(x)], buf.at[x], local.at[sem])
        mine.start()

        def finish():
            mine.wait()
            got.wait()
            return jnp.concatenate([buf[i].astype(f32) for i in range(NX)], axis=0).astype(bf16)

        return finish

    loads[4].wait()
    res_done = stage0(resv, raw, 6)
    loads[5].wait()
    tgt_done = stage0(tgtv, traw, 7)

    def blocks(buf, k, cw):
        def rows(first, n, xx, at=0, width=cw):
            return buf.at[
                pl.ds(pl.multiple_of(first, 16), n),
                pl.ds(pl.multiple_of(xx * SL + k * cw + at, 128), width),
            ]

        return rows

    def gather(buf, k, cw):
        rows = blocks(buf, k, cw)

        def like(n, width=cw):
            return buf.at[pl.ds(0, n), pl.ds(0, width)]

        def piece(zz):
            return rows(rows_c + zz * PR, PR, x)

        def side(hh, s, xx):
            return rows(rows_c + hh * HALF, HALF, xx, s * (cw // 2), cw // 2)

        zcr = Group(like(PR))
        z1 = [Group(like(PR)) for _ in range(3)]
        z2 = [Group(like(PR)) for _ in range(3)]
        xrt = [Group(like(HALF)) for _ in range(2)]
        xlt = [Group(like(HALF)) for _ in range(2)]
        fwd = [Group(like(HALF)) for _ in range(2)]
        o = 1 - h

        def ring(i, zz):
            xrt[i].go(right, piece(zz))
            xlt[i].go(left, piece(zz))

        def forward(i, hh):
            xrt[i].wait()
            fwd[i].go(right, side(hh, 0, xl))
            xlt[i].wait()
            fwd[i].go(left, side(hh, 1, xr))

        zcr.go(cross, piece(z))
        for d in range(3):
            z1[d].go(near_dev[d], piece(z))
        ring(0, z)
        for d in range(3):
            yield
            z1[d].wait()
            ring(0, near_z[d])
        yield
        zcr.wait()
        for d in (2, 1, 0):
            z2[d].go(near_dev[d], piece(zx))
        ring(1, zx)
        yield
        forward(0, h)
        for d in range(3):
            yield
            z2[d].wait()
            ring(1, lax.rem(near_z[d] + 4, NZ))
        yield
        forward(1, o)
        yield
        fwd[0].wait()
        yield
        fwd[1].wait()

    def gather2(buf, k, cw, hh):
        rows = blocks(buf, k, cw)

        def like(n, width=cw):
            return buf.at[pl.ds(0, n), pl.ds(0, width)]

        def piece(q):
            return rows(rows_c + hh * HALF + q * PR, PR, x)

        def all_of(xx, at=0, width=cw):
            return rows(rows_c + hh * HALF, HALF, xx, at, width)

        z1 = [Group(like(PR)) for _ in range(3)]
        xrt, xlt = Group(like(HALF)), Group(like(HALF))
        fwd = Group(like(HALF))
        mates = Group(like(HALF, NX * cw))

        def ring(q):
            xrt.go(right, piece(q))
            xlt.go(left, piece(q))

        for d in range(3):
            z1[d].go(near_dev[d], piece(zq))
        ring(zq)
        for d in range(3):
            yield
            z1[d].wait()
            ring(near_q[d])
        mates.go(mate, all_of(x))
        yield
        xrt.wait()
        fwd.go(right, all_of(xl, 0, cw // 2))
        xlt.wait()
        fwd.go(left, all_of(xr, cw // 2, cw // 2))
        mates.go(mate, all_of(xl))
        mates.go(mate, all_of(xr))
        yield
        fwd.wait()
        mates.go(mate, all_of(xo))
        yield
        mates.wait()

    mine = pl.ds(wrow, FD)
    loads[2].wait()
    half_tile = lax.broadcasted_iota(jnp.int32, (PR, FD), 0) < PR // 2
    mk[:, mine] = jnp.where(half_tile, mask[0].astype(f32), mask[1].astype(f32))
    loads[1].wait()
    we = Group(wencc.at[:, mine])
    we.go(mate, wencc.at[:, mine])
    loads[3].wait()
    wb = Group(bcat.at[:, mine], "odd")
    wb.go(mate, bcat.at[:, mine])
    wm = Group(mk.at[:, mine])
    wm.go(mate, mk.at[:, mine])
    loads[0].wait()
    wd = Group(wcat.at[mine])
    wd.go(mate, wcat.at[mine])

    first = res_done()
    g[pl.ds(pl.multiple_of(rows_c + z * PR, PR), PR), slab(x)] = first
    gathers = [gather(g, k, GW) for k in range(GCHUNKS)]

    def step(*gens):
        for gen in gens:
            next(gen, None)

    step(*gathers)

    tp[...] = tgt_done()
    shift = Group(tsh)
    shift.go(ys[3], tp, tsh)

    sq = jnp.zeros((FD, 128), f32)
    for q in range(0, D, 512):
        w = wcat[pl.ds(wrow, FD), q : q + 512].astype(f32)
        w = w * w
        sq = sq + (w[:, :128] + w[:, 128:256]) + (w[:, 256:384] + w[:, 384:])
    norm_col = jnp.sqrt(jnp.sum(sq, axis=1, keepdims=True) + norm_epsilon)
    norms[...] = jnp.broadcast_to(norm_col, (FD, FD)).T

    for _ in range(4):
        step(*gathers)

    shift.wait()
    swap1, swap2 = Group(tsw.at[0], "edge"), Group(tsw.at[1], "edge")
    edge = y == NY - 1

    @pl.when(edge)
    def _():
        swap1.go(up, tsh, tsw.at[0])

    for _ in range(4):
        step(*gathers)

    @pl.when(edge)
    def _():
        swap1.wait()
        swap2.go(up, tsw.at[0], tsw.at[1])

    def encode(hh):
        at = pl.multiple_of(hh * HALF, HALF)
        gx = g[pl.ds(pl.multiple_of(rows_c + at, HALF), HALF), :]
        pre = jnp.dot(gx, wencc[...], preferred_element_type=f32) + bcat[...]
        positive = jnp.maximum(pre, 0.0).reshape(HALF // PR, PR, NC * FD)
        keep = mk[...][None]
        here = pl.ds(at, HALF)
        actcat[here, :] = (keep * positive * positive).astype(bf16).reshape(HALF, NC * FD)
        p2cat[here, :] = (keep * 2.0 * positive).reshape(HALF, NC * FD)

    QUARTER = HALF // 2
    lo, hi = pl.ds(0, QUARTER), pl.ds(QUARTER, QUARTER)

    def reduce(i, hh):
        encode(hh)
        if i == 0:
            wd.wait()
        a = actcat[pl.ds(pl.multiple_of(hh * HALF, HALF), HALF), :]

        def decode(xx):
            return jnp.dot(a, wcat[:, slab(xx)], preferred_element_type=f32)

        o_r, o_l, direct, summed = (
            Group(opl.at[i]), Group(opr.at[i]), Group(inl.at[i]), Group(inl.at[i])
        )
        part[i, :, slab(xo)] = decode(xo).astype(bf16)
        o_r.go(right, part.at[i, lo, slab(xo)], opl.at[i])
        o_l.go(left, part.at[i, hi, slab(xo)], opr.at[i])
        part[i, :, slab(xr)] = decode(xr).astype(bf16)
        direct.go(right, part.at[i, hi, slab(xr)], inl.at[i, hi])
        part[i, :, slab(xl)] = decode(xl).astype(bf16)
        direct.go(left, part.at[i, lo, slab(xl)], inr.at[i, lo])
        own[i] = decode(x)
        yield
        o_r.wait()
        accr[i] = (part[i, lo, slab(xr)].astype(f32) + opl[i].astype(f32)).astype(bf16)
        summed.go(right, accr.at[i], inl.at[i, lo])
        o_l.wait()
        accl[i] = (part[i, hi, slab(xl)].astype(f32) + opr[i].astype(f32)).astype(bf16)
        summed.go(left, accl.at[i], inr.at[i, hi])
        yield
        direct.wait()
        summed.wait()
        total = own[i] + inl[i].astype(f32) + inr[i].astype(f32)
        ssum[i] = total
        sumb[i] = total.astype(bf16)

        def zrows(q):
            return pl.ds(pl.multiple_of(q * PR, PR), PR)

        parts = over[i]
        near = [Group(za.at[i, :, :, pl.ds(0, SL // len(parts))]) for _ in parts]
        w = SL // len(parts)
        for k in range(len(parts)):
            for d in (2, 1, 0):
                near[k].go(
                    near_dev[d],
                    sumb.at[i, zrows(near_q[d]), pl.ds(k * w, w)],
                    za.at[i, d, :, pl.ds(k * w, w)],
                )
        for k in range(len(parts)):
            yield
            near[k].wait()
            there = pl.ds(k * w, w)
            half_sum = ssum[i, zrows(zq), there]
            for d in range(3):
                half_sum = half_sum + za[i, d, :, there].astype(f32)
            zs[i, :, there] = half_sum.astype(bf16)
            parts[k].go(cross, zs.at[i, :, there], zc.at[1 - i, :, there])

    over = [
        [Group(zc.at[0])],
        [Group(zc.at[0, :, pl.ds(0, CW)]) for _ in range(CHUNKS)],
    ]
    early, late = reduce(0, h), reduce(1, 1 - h)

    step(*gathers)
    step(*gathers)
    we.wait()
    wb.wait()
    wm.wait()
    step(early)
    step(*gathers)
    step(early)
    step(late)
    other = pl.ds(orow, FD)
    these = pl.ds(pl.multiple_of(rows_c, CORE_ROWS), CORE_ROWS)
    gx = Group(g.at[these])
    gx.go(mate, g.at[these])
    ax, px = Group(act.at[these]), Group(pos2.at[these])
    ax.go(mate, actcat.at[:, other], act.at[these])
    px.go(mate, p2cat.at[:, other], pos2.at[these])

    @pl.when(edge)
    def _():
        swap2.wait()
        tfin[0] = tsw[1]
        sent(("edge",))

    @pl.when(y < NY - 1)
    def _():
        tfin[0] = tsh[...]

    tx = Group(tfin.at[0])
    tx.go(cross, tfin.at[0], tfin.at[1])
    act[these, :] = actcat[:, mine]
    pos2[these, :] = p2cat[:, mine]
    norm_row = norms[0:1, :]
    step(early)
    step(late)

    def transpose(first):
        for q in range(first, first + D // 2, 512):
            gt[q : q + 512, :] = g[:, q : q + 512].T

    gx.wait()
    transpose(0)
    step(late)
    ax.wait()
    px.wait()
    transpose(D // 2)
    step(early)
    act_t = act[...].T
    act_sum = jnp.sum(act_t.astype(f32), axis=1, keepdims=True)
    coef = penalty_weight * act_sum / norm_col
    lossb[0] = fold(act[...].astype(f32) * norm_row) * penalty_weight
    def finish(i, hh, k):
        there = slice(k * CW, (k + 1) * CW)
        recon = zs[i, :, there].astype(f32) + zc[i, :, there].astype(f32)
        misfit = recon - tfin[i, :, there].astype(f32)
        bk[
            pl.ds(pl.multiple_of(rows_c + (zq + 4 * hh) * PR, PR), PR),
            pl.ds(pl.multiple_of(x * SL + k * CW, CW), CW),
        ] = misfit.astype(bf16)
        if i == 1:
            lossb[0] = lossb[0] + fold(misfit * misfit) * 0.5

    def total_loss():
        par = lax.rem(zphys // 4, 2)
        xc = x * NC + c
        s1 = Group(lxc.at[pl.ds(0, 7)], "loss")
        lxc[xc] = lossb[0]
        for d in range(NX):
            for e in range(NC):
                if d or e:
                    device = dev(xx=lax.rem(x + d, NX), cc=c if not e else 1 - c)
                    s1.go(device, lxc.at[xc])
        yield
        s1.wait()
        cur = lxc[0]
        for i in range(1, NX * NC):
            cur = cur + lxc[i]
        for i, device in enumerate((far(4 + 8 * par), far(12 - 8 * par))):
            s2 = Group(lfar.at[2 * i], "loss")
            lfar[2 * i] = cur
            s2.go(device, lfar.at[2 * i], lfar.at[2 * i + 1])
            yield
            s2.wait()
            cur = cur + lfar[2 * i + 1]
        s3 = Group(lz.at[pl.ds(0, 3)], "loss")
        lz[zq] = cur
        for d in range(3):
            s3.go(near_dev[d], lz.at[zq])
        yield
        s3.wait()
        cur = (lz[0] + lz[1]) + (lz[2] + lz[3])
        s4 = Group(ly.at[pl.ds(0, 3)], "loss")
        ly[y] = cur
        for d in (1, 2, 3):
            s4.go(ys[d], ly.at[y])
        yield
        s4.wait()
        cur = (ly[0] + ly[1]) + (ly[2] + ly[3])
        loss_out[0, 0] = jnp.sum(cur) * scale

    loss_steps = total_loss()

    far_half = [gather2(bk, k, CW, 1 - h) for k in range(CHUNKS)]
    near_half = [gather2(bk, k, CW, h) for k in range(CHUNKS)]
    for k in range(CHUNKS):
        step(late)
    tx.wait()
    over[0][0].wait()
    for k in range(CHUNKS):
        finish(1, 1 - h, k)
        if k == CHUNKS - 1:
            step(loss_steps)
        step(far_half[k])

    def backward(k):
        for xx in range(NX):
            at = xx * SL + k * CW
            back = bk[:, at : at + CW]
            w = wcat[pl.ds(wrow, FD), at : at + CW]
            grad = jnp.dot(act_t, back, preferred_element_type=f32)
            dec_out[0, :, at : at + CW] = (grad + coef * w.astype(f32)).astype(bf16)
            more = contract_last(back, w)
            if k == 0 and xx == 0:
                actg[...] = more
            else:
                actg[...] += more

    step(*far_half)
    for k in range(CHUNKS):
        over[1][k].wait()
        finish(0, h, k)
        step(near_half[k])
    step(*far_half)
    step(loss_steps)
    step(*far_half)
    step(*far_half)
    step(*near_half)
    step(*near_half)
    step(*near_half)
    step(loss_steps)
    step(*far_half)
    step(*near_half)
    step(loss_steps)
    step(*near_half)
    step(*far_half)
    step(near_half[0])
    backward(0)
    step(loss_steps)
    for k in range(1, CHUNKS):
        step(near_half[k])
        backward(k)

    pre_grad = ((actg[...] + penalty_weight * norm_row) * pos2[...]).astype(bf16)
    bias_out[...] = jnp.sum(pre_grad.astype(f32), axis=0, keepdims=True)
    for q in range(0, D, 512):
        grad = jnp.dot(gt[q : q + 512, :], pre_grad, preferred_element_type=f32)
        enc_out[0, q : q + 512, :] = grad.astype(bf16)
    step(loss_steps)
    for gen in (*gathers, early, late, *far_half, *near_half, loss_steps):
        assert next(gen, "end") == "end"
    sent(("main", "odd", "loss"))
    assert (used[0], len(pools)) == (GROUPS, POOLS), (used, pools)


def write_out(*refs):
    sems = refs[8]
    pairs = []
    for src, dst in zip(refs[:4], refs[4:8]):
        rows = src.shape[1] // SPLIT if src.ndim == 3 else 0
        if rows:
            pairs += [(src.at[:, pl.ds(i * rows, rows)], dst.at[:, pl.ds(i * rows, rows)]) for i in range(SPLIT)]
        else:
            pairs.append((src, dst))
    copies = [pltpu.make_async_copy(src, dst, sems.at[i]) for i, (src, dst) in enumerate(pairs)]
    for copy in copies:
        copy.start()
    for copy in copies:
        copy.wait()


def body(residual, targets, w_enc, b_enc, w_dec, block_mask):
    scale = 1.0 / (lax.axis_size("layer") * TOKENS * D)
    hbm = pl.BlockSpec(memory_space=pltpu.HBM)
    vmem = pl.BlockSpec(memory_space=pltpu.VMEM)
    smem = pl.BlockSpec(memory_space=pltpu.SMEM)
    enc_grad, bias_grad, dec_grad, loss = pl.pallas_call(
        lambda *refs: kernel(scale, *refs),
        name="transcoder_step",
        out_shape=(
            jax.ShapeDtypeStruct((1, D, FD), bf16),
            jax.ShapeDtypeStruct((1, FD), f32),
            jax.ShapeDtypeStruct((1, FD, D), bf16),
            jax.ShapeDtypeStruct((1, 1), f32),
        ),
        in_specs=[hbm] * 6,
        out_specs=(vmem, vmem, vmem, smem),
        scratch_shapes=[
            pltpu.SMEM((2,), jnp.int32),
            pltpu.VMEM((1, NC * FD), f32),
            pltpu.VMEM((PR, NC * FD), f32),
            pltpu.VMEM((1, 4, D), bf16),
            pltpu.VMEM((1, 4, D), bf16),
            pltpu.VMEM((NX, 4, SL), bf16),
            pltpu.VMEM((NX, 4, SL), bf16),
            pltpu.VMEM((PR, SL), bf16),
            pltpu.VMEM((PR, SL), bf16),
            pltpu.VMEM((2, PR, SL), bf16),
            pltpu.VMEM((2, PR, SL), bf16),
            pltpu.VMEM((TOKENS, D), bf16),
            pltpu.VMEM((D, TOKENS), bf16),
            pltpu.VMEM((TOKENS, D), bf16),
            pltpu.VMEM((D, NC * FD), bf16),
            pltpu.VMEM((NC * FD, D), bf16),
            pltpu.VMEM((TOKENS, FD), bf16),
            pltpu.VMEM((CORE_ROWS, NC * FD), bf16),
            pltpu.VMEM((TOKENS, FD), f32),
            pltpu.VMEM((CORE_ROWS, NC * FD), f32),
            pltpu.VMEM((2, HALF, D), bf16),
            pltpu.VMEM((2, HALF, SL), f32),
            pltpu.VMEM((2, HALF // 2, SL), bf16),
            pltpu.VMEM((2, HALF // 2, SL), bf16),
            pltpu.VMEM((2, HALF // 2, SL), bf16),
            pltpu.VMEM((2, HALF // 2, SL), bf16),
            pltpu.VMEM((2, HALF, SL), bf16),
            pltpu.VMEM((2, HALF, SL), bf16),
            pltpu.VMEM((2, HALF, SL), bf16),
            pltpu.VMEM((2, HALF, SL), f32),
            pltpu.VMEM((2, 3, PR, SL), bf16),
            pltpu.VMEM((2, PR, SL), bf16),
            pltpu.VMEM((2, PR, SL), bf16),
            pltpu.VMEM((1, 8, 128), f32),
            pltpu.VMEM((NX * NC, 8, 128), f32),
            pltpu.VMEM((4, 8, 128), f32),
            pltpu.VMEM((4, 8, 128), f32),
            pltpu.VMEM((NY, 8, 128), f32),
            pltpu.VMEM((FD, FD), f32),
            pltpu.VMEM((TOKENS, FD), f32),
            pltpu.SemaphoreType.DMA((POOLS,)),
            pltpu.SemaphoreType.DMA((GROUPS,)),
            pltpu.SemaphoreType.DMA((8,)),
        ],
        compiler_params=pltpu.CompilerParams(
            collective_id=0, has_side_effects=True, vmem_limit_bytes=48 << 20
        ),
    )(*(pltpu.with_memory_space_constraint(a, pltpu.HBM) for a in (block_mask.reshape(2), residual, targets, w_enc, b_enc, w_dec)))
    results = (enc_grad, bias_grad, dec_grad, loss)
    enc_grad, bias_grad, dec_grad, loss = pl.pallas_call(
        write_out,
        name="write_out",
        out_shape=tuple(jax.ShapeDtypeStruct(r.shape, r.dtype) for r in results),
        in_specs=[pl.BlockSpec(memory_space=pl.ANY)] * 4,
        out_specs=(hbm,) * 4,
        scratch_shapes=[pltpu.SemaphoreType.DMA((2 * SPLIT + 2,))],
        compiler_params=pltpu.CompilerParams(vmem_limit_bytes=16 << 20),
    )(*results)
    return enc_grad, bias_grad, dec_grad, loss.reshape(())


def solution(mesh):
    return jax.shard_map(
        body,
        mesh=mesh,
        in_specs=(
            P("layer", "feat", None),
            P("layer", "feat", None),
            P("layer", None, "feat"),
            P("layer", "feat"),
            P("layer", "feat", None),
            P("layer", None, "feat"),
        ),
        out_specs=(P("layer", None, "feat"), P("layer", "feat"), P("layer", "feat", None), P()),
        check_vma=False,
    )
```

time: 85.4 us -> 80.8 us (0.946); the launches traced: 84.4 us -> 80.7 us
  Pallas kernels: 83.8 us -> 80.1 us
    pallas_call x1, Pallas kernels: 81.8 us -> 78.1 us  [body(): pl.pallas_call(lambda *refs: kernel(scale, *refs), name='transcoder_step'...]
where the time goes in v3:
time: 80.8 us; the launch traced here: 80.7 us
  Pallas kernels  80.1 us (99%)
    pallas_call x1, Pallas kernels, body(): pl.pallas_call(lambda *refs: kernel(scale, *refs), name='transcoder_step'...  78.1 us
    pallas_call x1, Pallas kernels, body(): pl.pallas_call(write_out, name='write_out', out_shape=tuple((jax.ShapeDty...  1.99 us

profile of v3, /device:TPU:1, one launch (start us, length us, event | category | flops | bytes accessed | tf_op | source)
XLA Modules:
  0.0 80.7 jit_solution(2564081752898074993)
XLA Ops:
  0.6 78.1 %transcoder_step.1 = (bf16[1,4096,128]{2,1,0:T(8,128)(2,1)S(1)}, f32[1,128]{1,0:T(1,128)S(1)}, bf16[1,128,4096]{2,1,0:T(8,128)(2,1)S(1)}, f32[1,1]{1,0:T(1,128)}) custom-call(s32[2]{0:T(128)} %bitcast.2, bf16[1,4,4096]{2,1,0:T(4,128)(2,1)} %refs_1_.1, bf16[1,4,4096]{2,1,0:T(4,128)(2,1)} %refs_2_.1, bf16[1,4096,128]{2,1,0:T(8,128)(2,1)} %refs_3_.1, ...), custom_call_target="tpu_custom_call" | custom-call | tf_op jit(solution)/shard_map/transcoder_step/pallas_call | solution.py:593
  78.7 2.0 %write_out.1 = (bf16[1,4096,128]{2,1,0:T(8,128)(2,1)}, f32[1,128]{1,0:T(1,128)}, bf16[1,128,4096]{2,1,0:T(8,128)(2,1)}, f32[1,1]{1,0:T(1,128)}) custom-call(bf16[1,4096,128]{2,1,0:T(8,128)(2,1)S(1)} %get-tuple-element.12.refs_0_, f32[1,128]{1,0:T(1,128)S(1)} %get-tuple-element.13.refs_1_, bf16[1,128,4096]{2,1,0:T(8,128)(2,1)S(1)} %get-tuple-element.14.refs_2_, ...), custom_call_target="tpu_custom_call" | custom-call | tf_op jit(solution)/shard_map/write_out/pallas_call | solution.py:654

commit v4 on v3

--- a/solution.py
+++ b/solution.py
@@ -13,11 +13,11 @@
 CORE_ROWS = TOKENS // NC
 HALF = CORE_ROWS // 2
 PR = CORE_ROWS // NZ
-GCHUNKS = 2
+GCHUNKS = 1
 GW = SL // GCHUNKS
 CHUNKS = 2
 CW = SL // CHUNKS
-GROUPS = 86
+GROUPS = 73
 POOLS = 11
 SPLIT = 1
 POOL = 1 << 20
@@ -218,12 +218,12 @@
         for d in (2, 1, 0):
             z2[d].go(near_dev[d], piece(zx))
         ring(1, zx)
-        yield
-        forward(0, h)
         for d in range(3):
             yield
             z2[d].wait()
             ring(1, lax.rem(near_z[d] + 4, NZ))
+        yield
+        forward(0, h)
         yield
         forward(1, o)
         yield
@@ -355,14 +355,22 @@
         o_r, o_l, direct, summed = (
             Group(opl.at[i]), Group(opr.at[i]), Group(inl.at[i]), Group(inl.at[i])
         )
+
+        def send_opposite():
+            o_r.go(right, part.at[i, lo, slab(xo)], opl.at[i])
+            o_l.go(left, part.at[i, hi, slab(xo)], opr.at[i])
+
         part[i, :, slab(xo)] = decode(xo).astype(bf16)
-        o_r.go(right, part.at[i, lo, slab(xo)], opl.at[i])
-        o_l.go(left, part.at[i, hi, slab(xo)], opr.at[i])
+        if i == 0:
+            send_opposite()
         part[i, :, slab(xr)] = decode(xr).astype(bf16)
+        part[i, :, slab(xl)] = decode(xl).astype(bf16)
+        own[i] = decode(x)
+        if i == 1:
+            yield
+            send_opposite()
         direct.go(right, part.at[i, hi, slab(xr)], inl.at[i, hi])
-        part[i, :, slab(xl)] = decode(xl).astype(bf16)
         direct.go(left, part.at[i, lo, slab(xl)], inr.at[i, lo])
-        own[i] = decode(x)
         yield
         o_r.wait()
         accr[i] = (part[i, lo, slab(xr)].astype(f32) + opl[i].astype(f32)).astype(bf16)
@@ -413,6 +421,7 @@
     wm.wait()
     step(early)
     step(*gathers)
+    step(late)
     step(early)
     step(late)
     other = pl.ds(orow, FD)

time: 80.8 us -> 79.5 us (0.984)
  Pallas kernels: 80.1 us -> 78.8 us
    pallas_call x1, Pallas kernels: 78.1 us -> 76.8 us  [body(): pl.pallas_call(lambda *refs: kernel(scale, *refs), name='transcoder_step'...]
where the time goes in v4:
time: 79.5 us; the launch traced here: 79.4 us
  Pallas kernels  78.8 us (99%)
    pallas_call x1, Pallas kernels, body(): pl.pallas_call(lambda *refs: kernel(scale, *refs), name='transcoder_step'...  76.8 us
    pallas_call x1, Pallas kernels, body(): pl.pallas_call(write_out, name='write_out', out_shape=tuple((jax.ShapeDty...  1.99 us

profile of v4, /device:TPU:1, one launch (start us, length us, event | category | flops | bytes accessed | tf_op | source)
XLA Modules:
  0.0 79.4 jit_solution(6932753872489587883)
XLA Ops:
  0.6 76.8 %transcoder_step.1 = (bf16[1,4096,128]{2,1,0:T(8,128)(2,1)S(1)}, f32[1,128]{1,0:T(1,128)S(1)}, bf16[1,128,4096]{2,1,0:T(8,128)(2,1)S(1)}, f32[1,1]{1,0:T(1,128)}) custom-call(s32[2]{0:T(128)} %bitcast.2, bf16[1,4,4096]{2,1,0:T(4,128)(2,1)} %refs_1_.1, bf16[1,4,4096]{2,1,0:T(4,128)(2,1)} %refs_2_.1, bf16[1,4096,128]{2,1,0:T(8,128)(2,1)} %refs_3_.1, ...), custom_call_target="tpu_custom_call" | custom-call | tf_op jit(solution)/shard_map/transcoder_step/pallas_call | solution.py:602
  77.4 2.0 %write_out.1 = (bf16[1,4096,128]{2,1,0:T(8,128)(2,1)}, f32[1,128]{1,0:T(1,128)}, bf16[1,128,4096]{2,1,0:T(8,128)(2,1)}, f32[1,1]{1,0:T(1,128)}) custom-call(bf16[1,4096,128]{2,1,0:T(8,128)(2,1)S(1)} %get-tuple-element.12.refs_0_, f32[1,128]{1,0:T(1,128)S(1)} %get-tuple-element.13.refs_1_, bf16[1,128,4096]{2,1,0:T(8,128)(2,1)S(1)} %get-tuple-element.14.refs_2_, ...), custom_call_target="tpu_custom_call" | custom-call | tf_op jit(solution)/shard_map/write_out/pallas_call | solution.py:663

commit v5 on v4

--- a/solution.py
+++ b/solution.py
@@ -456,11 +456,11 @@
 
     gx.wait()
     transpose(0)
+    step(early)
     step(late)
     ax.wait()
     px.wait()
     transpose(D // 2)
-    step(early)
     act_t = act[...].T
     act_sum = jnp.sum(act_t.astype(f32), axis=1, keepdims=True)
     coef = penalty_weight * act_sum / norm_col
@@ -559,9 +559,9 @@
     step(loss_steps)
     step(*near_half)
     step(*far_half)
+    step(loss_steps)
     step(near_half[0])
     backward(0)
-    step(loss_steps)
     for k in range(1, CHUNKS):
         step(near_half[k])
         backward(k)

time: 79.5 us -> 78.9 us (level)
  the two profiles are of different devices: /device:TPU:1 before, /device:TPU:4 now
where the time goes in v5:
time: 78.9 us; the launch traced here: 78.8 us
  Pallas kernels  78.1 us (99%)
    pallas_call x1, Pallas kernels, body(): pl.pallas_call(lambda *refs: kernel(scale, *refs), name='transcoder_step'...  76.1 us
    pallas_call x1, Pallas kernels, body(): pl.pallas_call(write_out, name='write_out', out_shape=tuple((jax.ShapeDty...  1.99 us

profile of v5, /device:TPU:4, one launch (start us, length us, event | category | flops | bytes accessed | tf_op | source)
XLA Modules:
  0.0 78.8 jit_solution(10343016424215272205)
XLA Ops:
  0.6 76.1 %transcoder_step.1 = (bf16[1,4096,128]{2,1,0:T(8,128)(2,1)S(1)}, f32[1,128]{1,0:T(1,128)S(1)}, bf16[1,128,4096]{2,1,0:T(8,128)(2,1)S(1)}, f32[1,1]{1,0:T(1,128)}) custom-call(s32[2]{0:T(128)} %bitcast.2, bf16[1,4,4096]{2,1,0:T(4,128)(2,1)} %refs_1_.1, bf16[1,4,4096]{2,1,0:T(4,128)(2,1)} %refs_2_.1, bf16[1,4096,128]{2,1,0:T(8,128)(2,1)} %refs_3_.1, ...), custom_call_target="tpu_custom_call" | custom-call | tf_op jit(solution)/shard_map/transcoder_step/pallas_call | solution.py:602
  76.8 2.0 %write_out.1 = (bf16[1,4096,128]{2,1,0:T(8,128)(2,1)}, f32[1,128]{1,0:T(1,128)}, bf16[1,128,4096]{2,1,0:T(8,128)(2,1)}, f32[1,1]{1,0:T(1,128)}) custom-call(bf16[1,4096,128]{2,1,0:T(8,128)(2,1)S(1)} %get-tuple-element.12.refs_0_, f32[1,128]{1,0:T(1,128)S(1)} %get-tuple-element.13.refs_1_, bf16[1,128,4096]{2,1,0:T(8,128)(2,1)S(1)} %get-tuple-element.14.refs_2_, ...), custom_call_target="tpu_custom_call" | custom-call | tf_op jit(solution)/shard_map/write_out/pallas_call | solution.py:663
